TPU v7x, 1024 devices: a whole 4x4x32 slice. The times are simulated.
1024 devices in a mesh: slab: 16 (over z_hi, x), dom: 64 (over z_lo, y, core).
Axes of the slice: x: 4, y: 4, z: 32 (z_hi: 4, z_lo: 8; z = z_hi * 8 + z_lo), core: 2. Of those that a mesh axis runs over, the one named last changes fastest.
Arguments:
- positions: float32 [3, 1048576], P(None, ('slab', 'dom')), may hold values from 0 to 64, as said below
- velocities: float32 [3, 1048576], P(None, ('slab', 'dom')), may hold values from -3 to 3
- mass: float32 [1048576], P(('slab', 'dom')), may hold values from 0.005 to 0.012
- smoothing: float32 [1048576], P(('slab', 'dom')), may hold values from 0.25 to 0.4
- energy: float32 [1048576], P(('slab', 'dom')), may hold values from 0.5 to 32, as said below
- send_offsets: int32 [4, 1024], P(None, ('slab', 'dom')), may hold values from 0 to 7, as said below
- send_counts: int32 [4, 1024], P(None, ('slab', 'dom')), may hold values from 1 to 8, as said below
- pair_blocks: int32 [8, 8192], P(None, ('slab', 'dom')), may hold values from 0 to 40, as said below
Outputs:
- density: float32 [1048576], P(('slab', 'dom'))
- acceleration: float32 [3, 1048576], P(None, ('slab', 'dom'))
- heating: float32 [1048576], P(('slab', 'dom'))
- step_share: float32 [1048576], P(('slab', 'dom'))
Inputs may be any that keep to these rules, and one draw needn't show every extreme that they name: `positions`: particle i of block g lies in the unit cube whose lowest corner is (slab index, domain index, local block index) of g. `energy`: largest near the middle of the box. `send_offsets`: offset plus count never passes 8. `send_counts`: some window holds all 8 blocks in every draw. `pair_blocks`: the first entry of each list is the block itself; an entry 8 (1 + r) + t names only a slot t below the count of the window received from direction r; 40 names no block; no other entry repeats within a list.
All inputs are finite; a program needn't handle non-finite values.
Results may differ from a plain program's by a relative error of at most 0.0003.
Values sent between devices are 32-bit elements; how exact they have to be, the bound alone decides.
A program may use at most 32 MiB of HBM per device.

v0:
```python
import math

import jax
import jax.numpy as jnp
from jax import lax
from jax.sharding import PartitionSpec as P

gas_gamma = 5.0 / 3.0
visc_alpha = 1.0
visc_beta = 2.0
courant = 0.4
index_pairs = ((0, 0), (1, 1), (2, 2), (0, 1), (0, 2), (1, 2))


def padded(value, sides, width):
    for axis, dim in sides:
        size, length = (lax.axis_size(axis), value.shape[dim])
        up = [(i, (i + 1) % size) for i in range(size - 1)]
        down = [(j, i) for i, j in up]
        last = lax.slice_in_dim(value, length - width, length, axis=dim)
        first = lax.slice_in_dim(value, 0, width, axis=dim)
        before = lax.ppermute(last, axis, up)
        after = lax.ppermute(first, axis, down)
        value = jnp.concatenate([before, value, after], axis=dim)
    return value


def kernel(distance, length):
    ratio = distance / length
    shape = 0.25 * jnp.maximum(2.0 - ratio, 0.0) ** 3 - jnp.maximum(1.0 - ratio, 0.0) ** 3
    return shape / (math.pi * length**3)


def apply_matrix(matrix, vector):
    return jnp.stack(
        [
            matrix[0] * vector[0] + matrix[3] * vector[1] + matrix[4] * vector[2],
            matrix[3] * vector[0] + matrix[1] * vector[1] + matrix[5] * vector[2],
            matrix[4] * vector[0] + matrix[5] * vector[1] + matrix[2] * vector[2],
        ]
    )


def block_density(pos_own, len_own, pos_near, mass_near):
    separation = pos_near[:, :, None] - pos_own[:, None, :]
    dist_sq = jnp.sum(separation * separation, axis=0)
    weight = mass_near[:, None] * kernel(jnp.sqrt(dist_sq), len_own[None, :])
    dens = jnp.sum(weight, axis=0)
    moments = [
        jnp.sum(weight * separation[first] * separation[second], axis=0) / dens
        for first, second in index_pairs
    ]
    floor = 0.05 * len_own * len_own
    axx = moments[0] + floor
    ayy = moments[1] + floor
    azz = moments[2] + floor
    axy, axz, ayz = (moments[3], moments[4], moments[5])
    cof_xx = ayy * azz - ayz * ayz
    cof_yy = axx * azz - axz * axz
    cof_zz = axx * ayy - axy * axy
    cof_xy = axz * ayz - axy * azz
    cof_xz = axy * ayz - ayy * axz
    cof_yz = axy * axz - axx * ayz
    determinant = axx * cof_xx + axy * cof_xy + axz * cof_xz
    matrix = jnp.stack([cof_xx, cof_yy, cof_zz, cof_xy, cof_xz, cof_yz]) / determinant
    return (dens, matrix)


def block_momentum(own_fields, near_fields):
    separation = near_fields[0:3, :, None] - own_fields[0:3, None, :]
    dist_sq = jnp.sum(separation * separation, axis=0)
    mean_len = 0.5 * (near_fields[7][:, None] + own_fields[7][None, :])
    kernel_val = kernel(jnp.sqrt(dist_sq), mean_len)
    grad_own = apply_matrix(own_fields[11:17, None, :], separation) * kernel_val
    grad_near = apply_matrix(near_fields[11:17, :, None], separation) * kernel_val
    grad_sum = grad_own + grad_near
    rel_vel = own_fields[4:7, None, :] - near_fields[4:7, :, None]
    closing = jnp.minimum(-jnp.sum(rel_vel * separation, axis=0), 0.0)
    closing_rate = mean_len * closing / (dist_sq + 0.01 * mean_len * mean_len)
    mean_sound = 0.5 * (own_fields[8][None, :] + near_fields[8][:, None])
    mean_dens = 0.5 * (own_fields[10][None, :] + near_fields[10][:, None])
    viscous = (
        -visc_alpha * mean_sound * closing_rate + visc_beta * closing_rate * closing_rate
    ) / mean_dens
    near_mass = near_fields[3][:, None]
    press_own = own_fields[9][None, :]
    press_near = near_fields[9][:, None]
    acceleration = -jnp.sum(
        near_mass * (press_own * grad_own + press_near * grad_near + 0.5 * viscous * grad_sum),
        axis=1,
    )
    heating = own_fields[9] * jnp.sum(near_mass * jnp.sum(rel_vel * grad_own, axis=0), axis=0)
    heating = heating + 0.25 * jnp.sum(
        near_mass * viscous * jnp.sum(rel_vel * grad_sum, axis=0), axis=0
    )
    signal = jnp.max(own_fields[8][None, :] + near_fields[8][:, None] - 3.0 * closing_rate, axis=0)
    return (acceleration, heating, signal)


def body(positions, velocities, mass, smoothing, energy, send_offsets, send_counts, pair_blocks):
    blocks = pair_blocks.shape[1]
    points = positions.shape[1] // blocks
    slots = jnp.arange(blocks, dtype=jnp.int32)
    chooser = (
        (slots[None, None, :] == send_offsets[:, :, None] + slots[None, :, None])
        & (slots[None, :, None] < send_counts[:, :, None])
    ).astype(jnp.float32)

    def windows(fields):
        shaped = fields.reshape(fields.shape[0], blocks, points)
        return jnp.einsum("rtb,fbk->rftk", chooser, shaped, precision=lax.Precision.HIGHEST)

    def assemble(local, from_slab, from_dom):
        shaped = local.reshape(local.shape[0], blocks, points)
        empty = jnp.zeros((local.shape[0], 1, points), jnp.float32)
        return jnp.concatenate(
            [shaped, from_slab[0], from_slab[3], from_dom[0], from_dom[3], empty], axis=1
        )

    def neighbours(table):
        picked = jnp.take(table, pair_blocks, axis=1)
        return picked.transpose(2, 0, 1, 3).reshape(blocks, table.shape[0], -1)

    def per_block(fields):
        return fields.reshape(fields.shape[0], blocks, points).transpose(1, 0, 2)

    sound = jnp.sqrt(gas_gamma * (gas_gamma - 1.0) * energy)
    first = jnp.concatenate([positions, mass[None]], axis=0)
    outgoing = windows(first)
    slab_first = padded(outgoing[0:2], (("slab", 0),), 1)
    dom_first = padded(outgoing[2:4], (("dom", 0),), 1)
    table_first = assemble(first, slab_first, dom_first)
    near_first = neighbours(table_first)

    def density_item(item):
        own_fields, near = item
        return block_density(own_fields[0:3], own_fields[3], near[0:3], near[3])

    own_first = per_block(jnp.concatenate([positions, smoothing[None]], axis=0))
    dens_parts, matrix_parts = lax.map(density_item, (own_first, near_first))
    density = dens_parts.reshape(-1)
    matrices = matrix_parts.transpose(1, 0, 2).reshape(6, -1)
    pressure = (gas_gamma - 1.0) * energy / density
    second = jnp.concatenate(
        [velocities, smoothing[None], sound[None], pressure[None], density[None], matrices], axis=0
    )
    outgoing_second = windows(second)
    slab_second = padded(outgoing_second[0:2], (("slab", 0),), 1)
    dom_second = padded(outgoing_second[2:4], (("dom", 0),), 1)
    table_second = assemble(second, slab_second, dom_second)
    near_all = neighbours(jnp.concatenate([table_first, table_second], axis=0))
    own_all = jnp.concatenate(
        [
            positions,
            mass[None],
            velocities,
            smoothing[None],
            sound[None],
            pressure[None],
            density[None],
            matrices,
        ],
        axis=0,
    )

    def momentum_item(item):
        own_fields, near = item
        return block_momentum(own_fields, near)

    accel_parts, heat_parts, signal_parts = lax.map(momentum_item, (per_block(own_all), near_all))
    acceleration = accel_parts.transpose(1, 0, 2).reshape(3, -1)
    heating = heat_parts.reshape(-1)
    allowed = courant * smoothing / signal_parts.reshape(-1)
    step = lax.pmin(jnp.min(allowed), ("slab", "dom"))
    return (density, acceleration, heating, step / allowed)


def solution(mesh):
    in_specs = (
        P(None, ("slab", "dom")),
        P(None, ("slab", "dom")),
        P(("slab", "dom")),
        P(("slab", "dom")),
        P(("slab", "dom")),
        P(None, ("slab", "dom")),
        P(None, ("slab", "dom")),
        P(None, ("slab", "dom")),
    )
    out_specs = (
        P(("slab", "dom")),
        P(None, ("slab", "dom")),
        P(("slab", "dom")),
        P(("slab", "dom")),
    )
    return jax.shard_map(body, mesh=mesh, in_specs=in_specs, out_specs=out_specs, check_vma=False)
```

profile of v0, /device:TPU:1, one launch (start us, length us, event | category | flops | bytes accessed | tf_op | source)
XLA Modules:
  0.0 305.1 jit_solution(4008954562162938490)
XLA Ops:
  0.6 0.7 iota_compare_fusion.1
  1.4 0.7 iota_add_fusion
  2.1 0.7 constant_dynamic-update-slice_fusion.29
  2.8 0.9 convolution_bitcast_fusion.1
  3.7 16.0 %collective-permute-start.3 = (f32[1,4,8,128]{3,2,1,0:T(8,128)S(1)}, f32[1,4,8,128]{3,2,1,0:T(8,128)S(1)}, u32[]{:S(2)}, u32[]{:S(2)}) collective-permute-start(f32[1,4,8,128]{3,2,1,0:T(8,128)S(1)} %get-tuple-element.246), channel_id=1, source_target_pairs={{1,0},{2,1},{3,2},{4,3},{5,4},{6,5},{7,6},{8,7},{9,8},{10,9},{11,1... | collective-permute-start | bytes 49160 | tf_op jit(solution)/shard_map/ppermute | solution.py:23
  19.8 1.9 collective-permute-start.2
  21.7 1.3 collective-permute-start.1
  23.0 4.0 %collective-permute-start = (f32[1,4,8,128]{3,2,1,0:T(8,128)S(1)}, f32[1,4,8,128]{3,2,1,0:T(8,128)S(1)}, u32[]{:S(2)}, u32[]{:S(2)}) collective-permute-start(f32[1,4,8,128]{3,2,1,0:T(8,128)S(1)} %get-tuple-element.249), channel_id=1, source_target_pairs={{0,64},{64,128},{128,192},{192,256},{256,320},{320,384},{384,448},... | collective-permute-start | bytes 49160 | tf_op jit(solution)/shard_map/ppermute | solution.py:22
  27.0 0.7 and_bitcast_fusion
  27.7 0.7 compare_select_fusion
  28.5 0.7 constant_dynamic-update-slice_fusion.28
  29.1 0.7 fusion.42
  29.8 0.7 constant_dynamic-update-slice_fusion.27
  30.6 0.7 constant_dynamic-update-slice_fusion.26
  31.3 0.7 constant_dynamic-update-slice_fusion.25
  32.1 0.7 gather_fusion
  33.0 11.3 %while.28 = (s32[]{:T(128)}, f32[8,128]{1,0:T(8,128)S(1)}, f32[8,6,128]{2,0,1:T(8,128)S(1)}, f32[8,4,1024]{2,1,0:T(4,128)S(1)}, f32[8,4,128]{2,0,1:T(8,128)S(1)}, /*index=5*/s32[]{:T(128)}, s32[]{:T(128)}, s32[]{}) while((s32[]{:T(128)}, f32[8,128]{1,0:T(8,128)S(1)}, f32[8,6,128]{2,0,1:T(8,128)S(1)}, f32[8,4,1024]{2,1,0:T(4,128)S(1)}, ...), condition=%wide.region_9.10_spmd, body=%wide.region_0.9_spmd.sunk | while | flops 4856067 | bytes 4299393 | solution.py:140
  33.6 0.6 multiply_reduce_fusion.14
  35.0 0.6 multiply_reduce_fusion.14
  36.4 0.6 multiply_reduce_fusion.14
  37.8 0.6 multiply_reduce_fusion.14
  39.2 0.6 multiply_reduce_fusion.14
  40.6 0.6 multiply_reduce_fusion.14
  42.0 0.6 multiply_reduce_fusion.14
  43.4 0.6 multiply_reduce_fusion.14
  44.6 1.9 collective-permute-start.4
  46.7 3.0 collective-permute-start.7
  49.6 2.6 collective-permute-start.6
  52.2 1.3 collective-permute-start.5
  53.6 4.1 %collective-permute-done.5 = f32[1,13,8,128]{3,2,1,0:T(8,128)S(1)} collective-permute-done((f32[1,13,8,128]{3,2,1,0:T(8,128)S(1)}, f32[1,13,8,128]{3,2,1,0:T(8,128)S(1)}, u32[]{:S(2)}, u32[]{:S(2)}) %collective-permute-start.5) | collective-permute-done | bytes 53280 | tf_op jit(solution)/shard_map/ppermute | solution.py:23
  58.0 0.6 gather_fusion.1
  59.1 51.4 %while.29 = (s32[]{:T(128)}, f32[8,3,128]{2,1,0:T(4,128)S(1)}, f32[8,128]{1,0:T(8,128)S(1)}, f32[8,128]{1,0:T(8,128)S(1)}, f32[8,17,1024]{2,0,1:T(8,128)S(1)}, /...) while((s32[]{:T(128)}, f32[8,3,128]{2,1,0:T(4,128)S(1)}, ...), condition=%wide.region_19.20_spmd, body=%wide.region_10.19_spmd.sunk | while | flops 21495820 | bytes 21317580 | solution.py:170
  60.3 1.0 multiply_add_fusion.11
  61.6 1.2 fusion.70
  63.3 1.7 fusion.71
  65.0 0.5 fusion.72
  66.7 1.0 multiply_add_fusion.11
  68.0 1.2 fusion.70
  69.7 1.7 fusion.71
  71.4 0.5 fusion.72
  73.2 1.0 multiply_add_fusion.11
  74.5 1.2 fusion.70
  76.1 1.7 fusion.71
  77.8 0.5 fusion.72
  79.6 1.0 multiply_add_fusion.11
  80.9 1.2 fusion.70
  82.5 1.7 fusion.71
  84.2 0.5 fusion.72
  86.0 1.0 multiply_add_fusion.11
  87.3 1.2 fusion.70
  89.0 1.7 fusion.71
  90.7 0.5 fusion.72
  92.5 1.0 multiply_add_fusion.11
  93.8 1.2 fusion.70
  95.4 1.7 fusion.71
  98.9 1.0 multiply_add_fusion.11
  100.2 1.2 fusion.70
  101.8 1.7 fusion.71
  105.3 1.0 multiply_add_fusion.11
  106.6 1.2 fusion.70
  108.3 1.7 fusion.71
  110.6 0.6 fusion.52
  111.2 192.6 %pmin.7 = f32[]{:T(128)} all-reduce(f32[]{:T(128)} %fusion.52), channel_id=1, replica_groups=mesh['slab'=16,'dom'=64] {'slab','dom'}, use_global_device_ids=true, to_apply=%region_21.22 | all-reduce | flops 1 | bytes 8 | tf_op jit(solution)/shard_map/pmin | solution.py:174
  303.8 1.3 fusion.53
  (276 shorter events, 23.8 us)
Async XLA Ops:
  3.7 28.3 %collective-permute-start.3 = (f32[1,4,8,128]{3,2,1,0:T(8,128)S(1)}, f32[1,4,8,128]{3,2,1,0:T(8,128)S(1)}, u32[]{:S(2)}, u32[]{:S(2)}) collective-permute-start(f32[1,4,8,128]{3,2,1,0:T(8,128)S(1)} %get-tuple-element.246), channel_id=1, source_target_pairs={{1,0},{2,1},{3,2},{4,3},{5,4},{6,5},{7,6},{8,7},{9,8},{10,9},{11,1... | collective-permute-start | bytes 49160 | tf_op jit(solution)/shard_map/ppermute | solution.py:23
  19.8 12.3 %collective-permute-start.2 = (f32[1,4,8,128]{3,2,1,0:T(8,128)S(1)}, f32[1,4,8,128]{3,2,1,0:T(8,128)S(1)}, u32[]{:S(2)}, u32[]{:S(2)}) collective-permute-start(f32[1,4,8,128]{3,2,1,0:T(8,128)S(1)} %get-tuple-element.247), channel_id=1, source_target_pairs={{0,1},{1,2},{2,3},{3,4},{4,5},{5,6},{6,7},{7,8},{8,9},{9,10},{10,1... | collective-permute-start | bytes 49160 | tf_op jit(solution)/shard_map/ppermute | solution.py:22
  21.7 10.3 %collective-permute-start.1 = (f32[1,4,8,128]{3,2,1,0:T(8,128)S(1)}, f32[1,4,8,128]{3,2,1,0:T(8,128)S(1)}, u32[]{:S(2)}, u32[]{:S(2)}) collective-permute-start(f32[1,4,8,128]{3,2,1,0:T(8,128)S(1)} %get-tuple-element.248), channel_id=1, source_target_pairs={{64,0},{128,64},{192,128},{256,192},{320,256},{384,320},{448,384},... | collective-permute-start | bytes 49160 | tf_op jit(solution)/shard_map/ppermute | solution.py:23
  23.0 9.0 %collective-permute-start = (f32[1,4,8,128]{3,2,1,0:T(8,128)S(1)}, f32[1,4,8,128]{3,2,1,0:T(8,128)S(1)}, u32[]{:S(2)}, u32[]{:S(2)}) collective-permute-start(f32[1,4,8,128]{3,2,1,0:T(8,128)S(1)} %get-tuple-element.249), channel_id=1, source_target_pairs={{0,64},{64,128},{128,192},{192,256},{256,320},{320,384},{384,448},... | collective-permute-start | bytes 49160 | tf_op jit(solution)/shard_map/ppermute | solution.py:22
  33.0 11.3 %copy-start.2 = (f32[1024]{0:T(1024)S(1)}, f32[1024]{0:T(1024)}, u32[]{:S(2)}) copy-start(f32[1024]{0:T(1024)} %param.16) | copy-start | bytes 12292
  44.3 14.4 %copy-start.1 = (f32[8,128]{1,0:T(8,128)}, f32[8,128]{1,0:T(8,128)S(1)}, u32[]{:S(2)}) copy-start(f32[8,128]{1,0:T(8,128)S(1)} %get-tuple-element.112) | copy-start | bytes 12292
  44.6 8.9 %collective-permute-start.4 = (f32[1,13,8,128]{3,2,1,0:T(8,128)S(1)}, f32[1,13,8,128]{3,2,1,0:T(8,128)S(1)}, u32[]{:S(2)}, u32[]{:S(2)}) collective-permute-start(f32[1,13,8,128]{3,2,1,0:T(8,128)S(1)} %get-tuple-element.245), channel_id=1, source_target_pairs={{0,64},{64,128},{128,192},{192,256},{256,320},{320,384},{384,448},... | collective-permute-start | bytes 159752 | tf_op jit(solution)/shard_map/ppermute | solution.py:22
  46.7 11.1 %collective-permute-start.7 = (f32[1,13,8,128]{3,2,1,0:T(8,128)S(1)}, f32[1,13,8,128]{3,2,1,0:T(8,128)S(1)}, u32[]{:S(2)}, u32[]{:S(2)}) collective-permute-start(f32[1,13,8,128]{3,2,1,0:T(8,128)S(1)} %get-tuple-element.242), channel_id=1, source_target_pairs={{1,0},{2,1},{3,2},{4,3},{5,4},{6,5},{7,6},{8,7},{9,8},{10,9},{11,1... | collective-permute-start | bytes 159752 | tf_op jit(solution)/shard_map/ppermute | solution.py:23
  49.6 8.1 %collective-permute-start.6 = (f32[1,13,8,128]{3,2,1,0:T(8,128)S(1)}, f32[1,13,8,128]{3,2,1,0:T(8,128)S(1)}, u32[]{:S(2)}, u32[]{:S(2)}) collective-permute-start(f32[1,13,8,128]{3,2,1,0:T(8,128)S(1)} %get-tuple-element.243), channel_id=1, source_target_pairs={{0,1},{1,2},{2,3},{3,4},{4,5},{5,6},{6,7},{7,8},{8,9},{9,10},{10,1... | collective-permute-start | bytes 159752 | tf_op jit(solution)/shard_map/ppermute | solution.py:22
  52.2 5.5 %collective-permute-start.5 = (f32[1,13,8,128]{3,2,1,0:T(8,128)S(1)}, f32[1,13,8,128]{3,2,1,0:T(8,128)S(1)}, u32[]{:S(2)}, u32[]{:S(2)}) collective-permute-start(f32[1,13,8,128]{3,2,1,0:T(8,128)S(1)} %get-tuple-element.244), channel_id=1, source_target_pairs={{64,0},{128,64},{192,128},{256,192},{320,256},{384,320},{448,384},... | collective-permute-start | bytes 159752 | tf_op jit(solution)/shard_map/ppermute | solution.py:23
  59.1 51.5 %copy-start = (f32[1024]{0:T(1024)S(1)}, f32[1024]{0:T(1024)}, u32[]{:S(2)}) copy-start(f32[1024]{0:T(1024)} %param.15) | copy-start | bytes 12292
  110.6 194.6 %copy-start.3 = (f32[8,128]{1,0:T(8,128)}, f32[8,128]{1,0:T(8,128)S(1)}, u32[]{:S(2)}) copy-start(f32[8,128]{1,0:T(8,128)S(1)} %get-tuple-element.115) | copy-start | bytes 12292
  110.6 194.6 %copy-start.4 = (f32[8,3,128]{2,1,0:T(4,128)}, f32[8,3,128]{2,1,0:T(4,128)S(1)}, u32[]{:S(2)}) copy-start(f32[8,3,128]{2,1,0:T(4,128)S(1)} %get-tuple-element.114) | copy-start | bytes 36868
where the time goes:
time: 306 us; the launch traced here: 305 us
  blocking collectives  193 us (63%)
  other arithmetic  64.6 us (21%)
  starting transfers between devices  32 us (10%)
  local copies, waits for them, and re-layouts  7.66 us (3%)
  waiting for transfers between devices  4.16 us (1%)
    pmin x1, blocking collectives, body(): step = lax.pmin(jnp.min(allowed), ('slab', 'dom'))  193 us
    ppermute x4, starting transfers between devices, padded(): after = lax.ppermute(first, axis, down)  21.6 us
    reduce_sum x8, other arithmetic, block_momentum(): jnp.sum(rel_vel * grad_sum, axis=0)  13.5 us
    ppermute x4, starting transfers between devices, padded(): before = lax.ppermute(last, axis, up)  10.4 us
    add x16, other arithmetic, apply_matrix(): matrix[0] * vector[0] + matrix[3] * vector[1] + matrix[4] * vector[2]  10.3 us
    reduce_sum x8, other arithmetic, block_momentum(): jnp.sum(rel_vel * grad_own, axis=0)  9.27 us
  transfers between devices with their start and end apart: 8, of which 1 were waited for; matrix products, arithmetic and copies ran while one was open for 2% of the time, Pallas kernels for 0%

commit v1 on v0

v1 whole, which is shorter than its diff:
```python
import functools
import math

import jax
import jax.numpy as jnp
from jax import lax
from jax.experimental import pallas as pl
from jax.experimental.pallas import tpu as pltpu
from jax.sharding import PartitionSpec as P

MESH = pl.DeviceIdType.MESH
GAMMA = 5.0 / 3.0
ROWS = 32
LANES = 128
BLOCKS = 8
TABLE = 41
NEAR_Z = 5
FAR_Z = 11


def recip(x):
    r = pl.reciprocal(x, approx=True)
    return r * (2.0 - x * r)


def fold(x):
    out = x[0:8]
    for k in range(8, x.shape[0], 8):
        out = out + x[k : k + 8]
    return out


def fold_max(x):
    out = x[0:8]
    for k in range(8, x.shape[0], 8):
        out = jnp.maximum(out, x[k : k + 8])
    return out


def kernel(
    pos, vel, mass, smo, ene, offs, pairs,
    dens_o, acc_o, heat_o, share_o,
    own_a, win_a, tab_m, own_b, win_b, send_a, send_m, send_b, jt_a, jt_b, allow, best, slots,
    sa, ra, sm, rm, sb, rb, ss, sr,
):
    s, d = lax.axis_index("slab"), lax.axis_index("dom")
    zh, x, zl, y, core = s // 4, s % 4, d // 8, (d // 2) % 4, d % 2
    z = zh * 8 + zl

    def device(z, x, y, core):
        return ((z // 8) * 4 + x, (z % 8) * 8 + y * 2 + core)

    halo = [
        ((s + 15) % 16, d, s > 0),
        ((s + 1) % 16, d, s < 15),
        (s, (d + 63) % 64, d > 0),
        (s, (d + 1) % 64, d < 63),
    ]
    plane = [device(z, (x + dx) % 4, y, (core + dc) % 2) for dx in range(4) for dc in range(2) if dx or dc]
    column = [device(z, x, (y + dy) % 4, core) for dy in range(1, 4)]
    near_z = [device((z + 32 + k) % 32, x, y, core) for n in range(1, NEAR_Z + 1) for k in (n, -n)]
    edge_z = [device((z + 32 + k) % 32, x, y, core) for k in (NEAR_Z + 1, -NEAR_Z - 1)]
    far_z = [device((z + 32 + k) % 32, x, y, core) for k in (FAR_Z, -FAR_Z)]

    barrier = pltpu.get_barrier_semaphore()
    for a, b, there in halo:
        @pl.when(there)
        def _():
            pl.semaphore_signal(barrier, inc=1, device_id=(a, b), device_id_type=MESH)
    greet = plane + column + near_z + edge_z
    for peer in greet:
        pl.semaphore_signal(barrier, inc=1, device_id=peer, device_id_type=MESH)

    for b in range(BLOCKS):
        cols = slice(b * LANES, (b + 1) * LANES)
        own_a[b, 0:3] = pos[:, cols]
        own_a[b, 3:6] = vel[:, cols]
        own_a[b, 6:7] = smo[b : b + 1]
        own_a[b, 7:8] = jnp.sqrt(GAMMA * (GAMMA - 1.0) * ene[b : b + 1])
    for r in range(4):
        for t in range(BLOCKS):
            src = jnp.minimum(offs[r, 0] + t, BLOCKS - 1)
            send_a[r, t] = own_a[src]
            send_m[r, t : t + 1] = mass[pl.ds(src, 1)]

    def to_columns(b, fields, masses):
        jt_a[b] = jnp.concatenate([fields, jnp.broadcast_to(masses, (8, LANES))], axis=0).T

    def own_columns(b, carry):
        to_columns(b, own_a[b], mass[pl.ds(b, 1)])
        return carry

    lax.fori_loop(0, BLOCKS, own_columns, 0)
    jt_a[TABLE - 1] = jnp.zeros((LANES, 16), jnp.float32)
    jt_b[TABLE - 1] = jnp.zeros((LANES, 8), jnp.float32)

    waits = len(greet) + jnp.where(s > 0, 1, 0) + jnp.where(s < 15, 1, 0) + jnp.where(d > 0, 1, 0) + jnp.where(d < 63, 1, 0)
    pl.semaphore_wait(barrier, waits)

    def copy(src, dst, send, recv, peer):
        return pltpu.make_async_remote_copy(
            src_ref=src, dst_ref=dst, send_sem=send, recv_sem=recv, device_id=peer, device_id_type=MESH
        )

    def window_copies(r, back):
        a, b, _ = halo[r]
        w = r if back else r ^ 1
        first = copy(send_a.at[r], win_a.at[pl.ds(8 * w, 8)], sa.at[r], ra.at[w], (a, b))
        masses = copy(send_m.at[r], tab_m.at[w], sm.at[r], rm.at[w], (a, b))
        return first, masses

    def second_copy(r, back):
        a, b, _ = halo[r]
        w = r if back else r ^ 1
        return copy(send_b.at[r], win_b.at[pl.ds(8 * w, 8)], sb.at[r], rb.at[w], (a, b))

    for r in range(4):
        @pl.when(halo[r][2])
        def _():
            for c in window_copies(r, False):
                c.start()
    for r in (2, 3, 0, 1):
        @pl.when(halo[r][2])
        def _():
            for c in window_copies(r, True):
                c.wait_recv()

        def columns(t, carry):
            to_columns(8 * (1 + r) + t, win_a[8 * r + t], tab_m[r, pl.ds(t, 1)])
            return carry

        lax.fori_loop(0, BLOCKS, columns, 0)

    def pair_loop(g, step, carry):
        def block(k, carry):
            e = pairs[k, g]
            for r0 in range(0, LANES, ROWS):
                carry = step(e, r0, carry)
            return carry

        return lax.fori_loop(0, BLOCKS, block, carry)

    def lane_rows(g):
        own = own_a[g]
        return [own[k : k + 1] for k in range(8)]

    zero = jnp.zeros((8, LANES), jnp.float32)

    def signal_block(g, carry):
        xi, yi, zi, ui, vi, wi, hi, ci = lane_rows(g)
        hi = 0.5 * hi

        def step(e, r0, top):
            j = jt_a[e, r0 : r0 + ROWS]
            sx, sy, sz = j[:, 0:1] - xi, j[:, 1:2] - yi, j[:, 2:3] - zi
            r2 = sx * sx + sy * sy + sz * sz
            us = (j[:, 3:4] - ui) * sx + (j[:, 4:5] - vi) * sy + (j[:, 5:6] - wi) * sz
            hb = 0.5 * j[:, 6:7] + hi
            mu = hb * jnp.minimum(us, 0.0) * recip(r2 + 0.01 * hb * hb)
            return jnp.maximum(top, fold_max(j[:, 7:8] - 3.0 * mu))

        top = pair_loop(g, step, jnp.full((8, LANES), -jnp.inf))
        top = jnp.max(top, axis=0, keepdims=True) + ci
        row = 0.4 * own_a[g, 6:7] / top
        allow[pl.ds(g, 1)] = row
        return jnp.minimum(carry, row)

    low = lax.fori_loop(0, BLOCKS, signal_block, jnp.full((1, LANES), jnp.inf))
    best[...] = low

    starts = {}
    base = 0
    for name, peers in (("plane", plane), ("column", column), ("near", near_z), ("far", far_z)):
        starts[name] = (base, peers)
        base += len(peers)

    def opposite(name, k):
        return k

    def reduce_copies(name):
        first, peers = starts[name]
        return [copy(best, slots.at[first + k], ss.at[first + k], sr.at[first + k], p) for k, p in enumerate(peers)]

    def reduce_start(name):
        for c in reduce_copies(name):
            c.start()

    def reduce_end(name):
        first, peers = starts[name]
        for c in reduce_copies(name):
            c.wait()
        low = best[...]
        for k in range(len(peers)):
            low = jnp.minimum(low, slots[first + k])
        best[...] = low

    reduce_start("plane")

    def density_block(g, carry):
        xi, yi, zi, _, _, _, hi, _ = lane_rows(g)
        inv = recip(hi)

        def step(e, r0, sums):
            j = jt_a[e, r0 : r0 + ROWS]
            sx, sy, sz = j[:, 0:1] - xi, j[:, 1:2] - yi, j[:, 2:3] - zi
            r2 = sx * sx + sy * sy + sz * sz
            q = r2 * lax.rsqrt(jnp.maximum(r2, 1e-30)) * inv
            a, b = jnp.maximum(2.0 - q, 0.0), jnp.maximum(1.0 - q, 0.0)
            w = j[:, 8:9] * (0.25 * a * a * a - b * b * b)
            wx, wy, wz = w * sx, w * sy, w * sz
            parts = (w, wx * sx, wy * sy, wz * sz, wx * sy, wx * sz, wy * sz)
            return tuple(t + fold(p) for t, p in zip(sums, parts))

        sums = pair_loop(g, step, (zero,) * 7)
        sums = [jnp.sum(t, axis=0, keepdims=True) for t in sums]
        dens = sums[0] * (inv * inv * inv * (1.0 / math.pi))
        per = 1.0 / sums[0]
        floor = 0.05 * hi * hi
        axx, ayy, azz = [t * per + floor for t in sums[1:4]]
        axy, axz, ayz = [t * per for t in sums[4:7]]
        cxx = ayy * azz - ayz * ayz
        cyy = axx * azz - axz * axz
        czz = axx * ayy - axy * axy
        cxy = axz * ayz - axy * azz
        cxz = axy * ayz - ayy * axz
        cyz = axy * axz - axx * ayz
        det = 1.0 / (axx * cxx + axy * cxy + axz * cxz)
        own_b[g, 0:1] = dens
        for k, v in enumerate((cxx, cyy, czz, cxy, cxz, cyz)):
            own_b[g, 1 + k : 2 + k] = v * det
        own_b[g, 7:8] = (GAMMA - 1.0) * ene[pl.ds(g, 1)] / dens
        dens_o[pl.ds(g, 1)] = dens
        jt_b[g] = own_b[g].T

        @pl.when(g == 1)
        def _():
            reduce_end("plane")
            reduce_start("column")

        @pl.when(g == 4)
        def _():
            reduce_end("column")
            reduce_start("near")

        return carry

    lax.fori_loop(0, BLOCKS, density_block, 0)

    for r in range(4):
        for t in range(BLOCKS):
            send_b[r, t] = own_b[jnp.minimum(offs[r, 0] + t, BLOCKS - 1)]
    for r in range(4):
        @pl.when(halo[r][2])
        def _():
            second_copy(r, False).start()
    reduce_end("near")
    reduce_start("far")
    for r in (2, 3, 0, 1):
        @pl.when(halo[r][2])
        def _():
            second_copy(r, True).wait_recv()

        def columns(t, carry):
            jt_b[8 * (1 + r) + t] = win_b[8 * r + t].T
            return carry

        lax.fori_loop(0, BLOCKS, columns, 0)

    def momentum_block(g, carry):
        xi, yi, zi, ui, vi, wi, hi, ci = lane_rows(g)
        hi, ci = 0.5 * hi, 0.5 * ci
        own = own_b[g]
        ri = 0.5 * own[0:1]
        cxx, cyy, czz, cxy, cxz, cyz, pi = [own[k : k + 1] for k in range(1, 8)]

        def step(e, r0, sums):
            j, k = jt_a[e, r0 : r0 + ROWS], jt_b[e, r0 : r0 + ROWS]
            sx, sy, sz = j[:, 0:1] - xi, j[:, 1:2] - yi, j[:, 2:3] - zi
            r2 = sx * sx + sy * sy + sz * sz
            ux, uy, uz = ui - j[:, 3:4], vi - j[:, 4:5], wi - j[:, 5:6]
            us = ux * sx + uy * sy + uz * sz
            hb = 0.5 * j[:, 6:7] + hi
            inv = recip(hb)
            q = r2 * lax.rsqrt(jnp.maximum(r2, 1e-30)) * inv
            a, b = jnp.maximum(2.0 - q, 0.0), jnp.maximum(1.0 - q, 0.0)
            w = (1.0 / math.pi) * j[:, 8:9] * (0.25 * a * a * a - b * b * b) * (inv * inv * inv)
            mu = hb * jnp.minimum(-us, 0.0) * recip(r2 + 0.01 * hb * hb)
            cb = 0.5 * j[:, 7:8] + ci
            half = 0.5 * w * mu * (2.0 * mu - cb) * recip(0.5 * k[:, 0:1] + ri)
            dxx, dyy, dzz, dxy, dxz, dyz = [k[:, n : n + 1] for n in range(1, 7)]
            tx = dxx * sx + dxy * sy + dxz * sz
            ty = dxy * sx + dyy * sy + dyz * sz
            tz = dxz * sx + dyz * sy + dzz * sz
            ox = cxx * sx + cxy * sy + cxz * sz
            oy = cxy * sx + cyy * sy + cyz * sz
            oz = cxz * sx + cyz * sy + czz * sz
            wp = w * pi
            one, two = wp + half, w * k[:, 7:8] + half
            parts = (
                one * ox + two * tx,
                one * oy + two * ty,
                one * oz + two * tz,
                (wp + 0.5 * half) * (ux * ox + uy * oy + uz * oz) + 0.5 * half * (ux * tx + uy * ty + uz * tz),
            )
            return tuple(t + fold(p) for t, p in zip(sums, parts))

        sums = pair_loop(g, step, (zero,) * 4)
        sums = [jnp.sum(t, axis=0, keepdims=True) for t in sums]
        cols = pl.ds(pl.multiple_of(g * LANES, LANES), LANES)
        for k in range(3):
            acc_o[k : k + 1, cols] = -sums[k]
        heat_o[pl.ds(g, 1)] = sums[3]
        return carry

    lax.fori_loop(0, BLOCKS, momentum_block, 0)

    reduce_end("far")
    share_o[...] = jnp.min(best[...], axis=1, keepdims=True) / allow[...]

    for r in range(4):
        @pl.when(halo[r][2])
        def _():
            for c in window_copies(r, False):
                c.wait_send()
            second_copy(r, False).wait_send()


def body(positions, velocities, mass, smoothing, energy, send_offsets, send_counts, pair_blocks):
    tile = (BLOCKS, LANES)
    vmem, smem = pl.BlockSpec(memory_space=pltpu.VMEM), pl.BlockSpec(memory_space=pltpu.SMEM)
    f32 = jnp.float32
    dma = pltpu.SemaphoreType.DMA
    n_slots = 7 + 3 + 2 * NEAR_Z + 2
    dens, acc, heat, share = pl.pallas_call(
        kernel,
        out_shape=(
            jax.ShapeDtypeStruct(tile, f32),
            jax.ShapeDtypeStruct(positions.shape, f32),
            jax.ShapeDtypeStruct(tile, f32),
            jax.ShapeDtypeStruct(tile, f32),
        ),
        in_specs=[vmem] * 5 + [smem] * 2,
        out_specs=(vmem,) * 4,
        scratch_shapes=[
            pltpu.VMEM((8, 8, LANES), f32),
            pltpu.VMEM((32, 8, LANES), f32),
            pltpu.VMEM((4, 8, LANES), f32),
            pltpu.VMEM((8, 8, LANES), f32),
            pltpu.VMEM((32, 8, LANES), f32),
            pltpu.VMEM((4, 8, 8, LANES), f32),
            pltpu.VMEM((4, 8, LANES), f32),
            pltpu.VMEM((4, 8, 8, LANES), f32),
            pltpu.VMEM((TABLE, LANES, 16), f32),
            pltpu.VMEM((TABLE, LANES, 8), f32),
            pltpu.VMEM(tile, f32),
            pltpu.VMEM((1, LANES), f32),
            pltpu.VMEM((n_slots, 1, LANES), f32),
            dma((4,)), dma((4,)), dma((4,)), dma((4,)), dma((4,)), dma((4,)),
            dma((n_slots,)), dma((n_slots,)),
        ],
        compiler_params=pltpu.CompilerParams(collective_id=0, has_side_effects=True),
        name="sph",
    )(
        positions, velocities, mass.reshape(tile), smoothing.reshape(tile), energy.reshape(tile),
        send_offsets, pair_blocks,
    )
    return dens.reshape(-1), acc, heat.reshape(-1), share.reshape(-1)


def solution(mesh):
    many = P(None, ("slab", "dom"))
    flat = P(("slab", "dom"))
    return jax.shard_map(
        body,
        mesh=mesh,
        in_specs=(many, many, flat, flat, flat, many, many, many),
        out_specs=(flat, many, flat, flat),
        check_vma=False,
    )
```

time: 306 us -> 116 us (0.38)
  the two profiles are of different devices: /device:TPU:1 before, /device:TPU:38 now
where the time goes in v1:
time: 116 us; the launch traced here: 115 us
  Pallas kernels  110 us (95%)
  local copies, waits for them, and re-layouts  4.54 us (4%)
    pallas_call x1, Pallas kernels, body(): pl.pallas_call(kernel, out_shape=(jax.ShapeDtypeStruct(tile, f32), jax.Sh...  110 us
    unnamed x13, local copies, waits for them, and re-layouts  4.54 us

profile of v1, /device:TPU:38, one launch (start us, length us, event | category | flops | bytes accessed | tf_op | source)
XLA Modules:
  0.0 115.3 jit_solution(3431887591473687676)
XLA Ops:
  0.6 0.0 copy-start.3
  0.6 0.6 copy-done.3
  1.3 0.7 copy.11.offs
  1.9 110.1 %sph.1 = (f32[8,128]{1,0:T(8,128)}, f32[3,1024]{1,0:T(4,128)}, f32[8,128]{1,0:T(8,128)}, f32[8,128]{1,0:T(8,128)}) custom-call(f32[3,1024]{1,0:T(4,128)} %pos.1, f32[3,1024]{1,0:T(4,128)} %vel.1, f32[8,128]{1,0:T(8,128)} %bitcast.6, f32[8,128]{1,0:T(8,128)} %bitcast.7, f32[8,128]{1,0:T(8,128)} %bitcast.8, s32[4,1]{1,0:T(4,128)} %copy.11.offs, s32[8,8]{1,0:T(8,128)} %pairs.1), custom_call_target="tpu_custom_call" | custom-call | tf_op jit(solution)/shard_map/sph/pallas_call | solution.py:334
  112.1 0.0 copy-start
  112.1 1.3 %copy.16 = f32[1024]{0:T(1024)} copy(f32[1024]{0:T(1024)} %bitcast.11) | data formatting | bytes 8192
  113.4 0.0 copy-done
  113.4 0.0 copy-start.2
  113.4 0.6 copy.17
  114.0 0.1 copy-done.2
  114.1 0.0 copy-start.1
  114.1 0.6 copy.18
  114.7 0.1 copy-done.1
  114.7 0.6 copy.19
Async XLA Ops:
  0.6 0.7 copy-start.3
  112.1 1.3 %copy-start = (f32[3,1024]{1,0:T(4,128)S(1)}, f32[3,1024]{1,0:T(4,128)}, u32[]{:S(2)}) copy-start(f32[3,1024]{1,0:T(4,128)} %get-tuple-element.17) | copy-start | bytes 36868
  113.4 0.7 copy-start.2
  114.1 0.7 copy-start.1

commit v2 on v1

v2 whole, which is shorter than its diff:
```python
import functools
import math

import jax
import jax.numpy as jnp
from jax import lax
from jax.experimental import pallas as pl
from jax.experimental.pallas import tpu as pltpu
from jax.sharding import PartitionSpec as P

MESH = pl.DeviceIdType.MESH
GAMMA = 5.0 / 3.0
CHUNK = 4
UNROLL = 8
PARTS = 4
LANES = 128
BLOCKS = 8
TABLE = 41
NEAR_Z = 5
FAR_Z = 11


def recip(x):
    r = pl.reciprocal(x, approx=True)
    return r * (2.0 - x * r)


def kernel(
    pos, vel, mass, smo, ene, offs, pairs,
    dens_o, acc_o, heat_o, share_o,
    own_a, win_a, tab_m, own_b, win_b, send_a, send_m, send_b, near_a, near_b, self_a, self_b, kept, early, tile, allow, best, slots,
    sa, ra, sm, rm, sb, rb, ss, sr,
):
    s, d = lax.axis_index("slab"), lax.axis_index("dom")
    zh, x, zl, y, core = s // 4, s % 4, d // 8, (d // 2) % 4, d % 2
    z = zh * 8 + zl

    def device(z, x, y, core):
        return ((z // 8) * 4 + x, (z % 8) * 8 + y * 2 + core)

    halo = [
        ((s + 15) % 16, d, s > 0),
        ((s + 1) % 16, d, s < 15),
        (s, (d + 63) % 64, d > 0),
        (s, (d + 1) % 64, d < 63),
    ]
    plane = [device(z, (x + dx) % 4, y, (core + dc) % 2) for dx in range(4) for dc in range(2) if dx or dc]
    column = [device(z, x, (y + dy) % 4, core) for dy in range(1, 4)]
    near_z = [device((z + 32 + k) % 32, x, y, core) for n in range(1, NEAR_Z + 1) for k in (n, -n)]
    edge_z = [device((z + 32 + k) % 32, x, y, core) for k in (NEAR_Z + 1, -NEAR_Z - 1)]
    far_z = [device((z + 32 + k) % 32, x, y, core) for k in (FAR_Z, -FAR_Z)]

    barrier = pltpu.get_barrier_semaphore()
    for a, b, there in halo:
        @pl.when(there)
        def _():
            pl.semaphore_signal(barrier, inc=1, device_id=(a, b), device_id_type=MESH)
    greet = plane + column + near_z + edge_z
    for peer in greet:
        pl.semaphore_signal(barrier, inc=1, device_id=peer, device_id_type=MESH)

    for b in range(BLOCKS):
        cols = slice(b * LANES, (b + 1) * LANES)
        own_a[b, 0:3] = pos[:, cols]
        own_a[b, 3:6] = vel[:, cols]
        own_a[b, 6:7] = 0.5 * smo[b : b + 1]
        own_a[b, 7:8] = 0.5 * jnp.sqrt(GAMMA * (GAMMA - 1.0) * ene[b : b + 1])
    for r in range(4):
        for t in range(BLOCKS):
            src = jnp.minimum(offs[r, 0] + t, BLOCKS - 1)
            send_a[r, t] = own_a[src]
            send_m[r, t : t + 1] = mass[pl.ds(src, 1)]

    def spread_first(b, fields, masses):
        for f in range(8):
            near_a[b, f] = jnp.broadcast_to(fields[f : f + 1], (8, LANES))
        near_a[b, 8] = jnp.broadcast_to(masses, (8, LANES))

    def spread_second(b, fields):
        for f in range(8):
            near_b[b, f] = jnp.broadcast_to(fields[f : f + 1], (8, LANES))

    def across(rows, f):
        return jnp.broadcast_to(rows[:, f : f + 1], (LANES, LANES)).reshape(16, 8, LANES)

    def own_first(b, carry):
        fields = own_a[b]
        spread_first(b, fields, mass[pl.ds(b, 1)])
        columns = fields.T
        for f in range(8):
            self_a[b, f] = across(columns, f)
        self_a[b, 8] = across(recip(2.0 * columns[:, 6:7]), 0)
        return carry

    lax.fori_loop(0, BLOCKS, own_first, 0)
    near_a[TABLE - 1] = jnp.zeros((9, 8, LANES), jnp.float32)
    near_b[TABLE - 1] = jnp.zeros((8, 8, LANES), jnp.float32)
    lane = lax.broadcasted_iota(jnp.int32, (CHUNK, 8, LANES), 2)

    waits = len(greet) + jnp.where(s > 0, 1, 0) + jnp.where(s < 15, 1, 0) + jnp.where(d > 0, 1, 0) + jnp.where(d < 63, 1, 0)
    pl.semaphore_wait(barrier, waits)

    def copy(src, dst, send, recv, peer):
        return pltpu.make_async_remote_copy(
            src_ref=src, dst_ref=dst, send_sem=send, recv_sem=recv, device_id=peer, device_id_type=MESH
        )

    def window_copies(r, back):
        a, b, _ = halo[r]
        w = r if back else r ^ 1
        first = copy(send_a.at[r], win_a.at[pl.ds(8 * w, 8)], sa.at[r], ra.at[w], (a, b))
        masses = copy(send_m.at[r], tab_m.at[w], sm.at[r], rm.at[w], (a, b))
        return first, masses

    def second_copy(r, back):
        a, b, _ = halo[r]
        w = r if back else r ^ 1
        return copy(send_b.at[r], win_b.at[pl.ds(8 * w, 8)], sb.at[r], rb.at[w], (a, b))

    for r in range(4):
        @pl.when(halo[r][2])
        def _():
            for c in window_copies(r, False):
                c.start()
    for r in (2, 3, 0, 1):
        @pl.when(halo[r][2])
        def _():
            for c in window_copies(r, True):
                c.wait_recv()

        def arrived(t, carry):
            spread_first(8 * (1 + r) + t, win_a[8 * r + t], tab_m[r, pl.ds(t, 1)])
            return carry

        lax.fori_loop(0, BLOCKS, arrived, 0)

    def pair_sums(g, count, start, make, collect):
        def part(at):
            step = make(at)

            def block(k, sums):
                for i in range(UNROLL):
                    sums = step(pairs[k * UNROLL + i, g], k * UNROLL + i, sums)
                return sums

            zero = jnp.full((CHUNK, 8, LANES), start, jnp.float32)
            sums = lax.fori_loop(0, BLOCKS // UNROLL, block, (zero,) * count)
            out = jnp.zeros((CHUNK, 8, LANES), jnp.float32)
            for q, t in enumerate(sums):
                out = jnp.where(lane == q, collect(t, axis=2, keepdims=True), out)
            tile[at] = out

        def chunk(n, carry):
            for i in range(PARTS):
                part(pl.ds((n * PARTS + i) * CHUNK, CHUNK))
            return carry

        lax.fori_loop(0, 16 // (PARTS * CHUNK), chunk, 0)
        rows = tile[...].reshape(LANES, LANES).T
        return [rows[q : q + 1] for q in range(count)]

    def signal_block(g, carry):
        def make(at):
            def step(e, k, sums):
                sx, sy, sz = [near_a[e, f] - self_a[g, f, at] for f in range(3)]
                ux, uy, uz = [near_a[e, f] - self_a[g, f, at] for f in range(3, 6)]
                r2 = sx * sx + sy * sy + sz * sz
                us = ux * sx + uy * sy + uz * sz
                hb = near_a[e, 6] + self_a[g, 6, at]
                mu = hb * jnp.minimum(us, 0.0) * recip(r2 + 0.01 * hb * hb)
                kept[g, k, 0, at] = r2
                kept[g, k, 1, at] = mu
                return (jnp.maximum(sums[0], near_a[e, 7] - 1.5 * mu),)

            return step

        (top,) = pair_sums(g, 1, -jnp.inf, make, jnp.max)
        row = 0.4 * own_a[g, 6:7] / (top + own_a[g, 7:8])
        allow[pl.ds(g, 1)] = row
        return jnp.minimum(carry, row)

    low = lax.fori_loop(0, BLOCKS, signal_block, jnp.full((1, LANES), jnp.inf))
    best[...] = low

    starts = {}
    base = 0
    for name, peers in (("plane", plane), ("column", column), ("near", near_z), ("far", far_z)):
        starts[name] = (base, peers)
        base += len(peers)

    def opposite(name, k):
        return k

    def reduce_copies(name):
        first, peers = starts[name]
        return [copy(best, slots.at[first + k], ss.at[first + k], sr.at[first + k], p) for k, p in enumerate(peers)]

    def reduce_start(name):
        for c in reduce_copies(name):
            c.start()

    def reduce_end(name):
        first, peers = starts[name]
        for c in reduce_copies(name):
            c.wait()
        low = best[...]
        for k in range(len(peers)):
            low = jnp.minimum(low, slots[first + k])
        best[...] = low

    reduce_start("plane")

    def density_block(g, carry):
        hi = 2.0 * own_a[g, 6:7]
        inv = recip(hi)
        def make(at):
            def step(e, k, sums):
                sx, sy, sz = [near_a[e, f] - self_a[g, f, at] for f in range(3)]
                r2 = kept[g, k, 0, at]
                q = r2 * lax.rsqrt(jnp.maximum(r2, 1e-30)) * self_a[g, 8, at]
                a, b = jnp.maximum(2.0 - q, 0.0), jnp.maximum(1.0 - q, 0.0)
                w = near_a[e, 8] * (0.25 * a * a * a - b * b * b)
                wx, wy, wz = w * sx, w * sy, w * sz
                parts = (w, wx * sx, wy * sy, wz * sz, wx * sy, wx * sz, wy * sz)
                return tuple(t + p for t, p in zip(sums, parts))

            return step

        sums = pair_sums(g, 7, 0.0, make, jnp.sum)
        dens = sums[0] * (inv * inv * inv * (1.0 / math.pi))
        per = 1.0 / sums[0]
        floor = 0.05 * hi * hi
        axx, ayy, azz = [t * per + floor for t in sums[1:4]]
        axy, axz, ayz = [t * per for t in sums[4:7]]
        cxx = ayy * azz - ayz * ayz
        cyy = axx * azz - axz * axz
        czz = axx * ayy - axy * axy
        cxy = axz * ayz - axy * azz
        cxz = axy * ayz - ayy * axz
        cyz = axy * axz - axx * ayz
        det = 1.0 / (axx * cxx + axy * cxy + axz * cxz)
        own_b[g, 0:1] = dens
        for k, v in enumerate((cxx, cyy, czz, cxy, cxz, cyz)):
            own_b[g, 1 + k : 2 + k] = v * det
        own_b[g, 7:8] = (GAMMA - 1.0) * ene[pl.ds(g, 1)] / dens
        dens_o[pl.ds(g, 1)] = dens
        spread_second(g, own_b[g])

        @pl.when(g == 2)
        def _():
            reduce_end("plane")
            reduce_start("column")

        @pl.when(g == 5)
        def _():
            reduce_end("column")
            reduce_start("near")

        return carry

    lax.fori_loop(0, BLOCKS, density_block, 0)

    for r in range(4):
        for t in range(BLOCKS):
            send_b[r, t] = own_b[jnp.minimum(offs[r, 0] + t, BLOCKS - 1)]
    for r in range(4):
        @pl.when(halo[r][2])
        def _():
            second_copy(r, False).start()

    def early_block(g, carry):
        columns = own_b[g].T
        for f in range(7):
            self_b[g, f] = across(columns, f)

        def make(at):
            def step(e, k, sums):
                sx, sy, sz = [near_a[e, f] - self_a[g, f, at] for f in range(3)]
                ux, uy, uz = [near_a[e, f] - self_a[g, f, at] for f in range(3, 6)]
                r2, mu = kept[g, k, 0, at], kept[g, k, 1, at]
                hb = near_a[e, 6] + self_a[g, 6, at]
                inv = recip(hb)
                q = r2 * lax.rsqrt(jnp.maximum(r2, 1e-30)) * inv
                a, b = jnp.maximum(2.0 - q, 0.0), jnp.maximum(1.0 - q, 0.0)
                w = near_a[e, 8] * (0.25 * a * a * a - b * b * b) * (inv * inv * inv)
                cb = near_a[e, 7] + self_a[g, 7, at]
                cxx, cyy, czz, cxy, cxz, cyz = [self_b[g, f, at] for f in range(1, 7)]
                ox = cxx * sx + cxy * sy + cxz * sz
                oy = cxy * sx + cyy * sy + cyz * sz
                oz = cxz * sx + cyz * sy + czz * sz
                uo = ux * ox + uy * oy + uz * oz
                kept[g, k, 0, at] = w
                kept[g, k, 1, at] = w * mu * (2.0 * mu - cb)
                kept[g, k, 2, at] = uo
                return tuple(t + p for t, p in zip(sums, (w * sx, w * sy, w * sz, w * uo)))

            return step

        for q, row in enumerate(pair_sums(g, 4, 0.0, make, jnp.sum)):
            early[g, q : q + 1] = row

        @pl.when(g == 1)
        def _():
            reduce_end("near")
            reduce_start("far")

        return carry

    lax.fori_loop(0, BLOCKS, early_block, 0)
    for r in (2, 3, 0, 1):
        @pl.when(halo[r][2])
        def _():
            second_copy(r, True).wait_recv()

        def arrived(t, carry):
            spread_second(8 * (1 + r) + t, win_b[8 * r + t])
            return carry

        lax.fori_loop(0, BLOCKS, arrived, 0)

    def momentum_block(g, carry):
        def make(at):
            def step(e, k, sums):
                sx, sy, sz = [near_a[e, f] - self_a[g, f, at] for f in range(3)]
                ux, uy, uz = [near_a[e, f] - self_a[g, f, at] for f in range(3, 6)]
                w, viscous, uo = [kept[g, k, n, at] for n in range(3)]
                half = viscous * recip(near_b[e, 0] + self_b[g, 0, at])
                dxx, dyy, dzz, dxy, dxz, dyz = [near_b[e, f] for f in range(1, 7)]
                tx = dxx * sx + dxy * sy + dxz * sz
                ty = dxy * sx + dyy * sy + dyz * sz
                tz = dxz * sx + dyz * sy + dzz * sz
                two = w * near_b[e, 7] + half
                work = uo + (ux * tx + uy * ty + uz * tz)
                parts = (two * tx, two * ty, two * tz, half * sx, half * sy, half * sz, half * work)
                return tuple(t + p for t, p in zip(sums, parts))

            return step

        late = pair_sums(g, 7, 0.0, make, jnp.sum)
        own = own_b[g]
        cxx, cyy, czz, cxy, cxz, cyz, pi = [own[f : f + 1] for f in range(1, 8)]
        px, py, pz, pw = [pi * early[g, q : q + 1] for q in range(4)]
        px, py, pz = px + late[3], py + late[4], pz + late[5]
        sums = [
            cxx * px + cxy * py + cxz * pz + late[0],
            cxy * px + cyy * py + cyz * pz + late[1],
            cxz * px + cyz * py + czz * pz + late[2],
            -pw - 0.5 * late[6],
        ]
        sums = [t * (1.0 / math.pi) for t in sums]
        cols = pl.ds(pl.multiple_of(g * LANES, LANES), LANES)
        for k in range(3):
            acc_o[k : k + 1, cols] = -sums[k]
        heat_o[pl.ds(g, 1)] = sums[3]
        return carry

    lax.fori_loop(0, BLOCKS, momentum_block, 0)

    reduce_end("far")
    share_o[...] = jnp.min(best[...], axis=1, keepdims=True) / allow[...]

    for r in range(4):
        @pl.when(halo[r][2])
        def _():
            for c in window_copies(r, False):
                c.wait_send()
            second_copy(r, False).wait_send()


def body(positions, velocities, mass, smoothing, energy, send_offsets, send_counts, pair_blocks):
    shape = (BLOCKS, LANES)
    vmem, smem = pl.BlockSpec(memory_space=pltpu.VMEM), pl.BlockSpec(memory_space=pltpu.SMEM)
    f32 = jnp.float32
    dma = pltpu.SemaphoreType.DMA
    n_slots = 7 + 3 + 2 * NEAR_Z + 2
    dens, acc, heat, share = pl.pallas_call(
        kernel,
        out_shape=(
            jax.ShapeDtypeStruct(shape, f32),
            jax.ShapeDtypeStruct(positions.shape, f32),
            jax.ShapeDtypeStruct(shape, f32),
            jax.ShapeDtypeStruct(shape, f32),
        ),
        in_specs=[vmem] * 5 + [smem] * 2,
        out_specs=(vmem,) * 4,
        scratch_shapes=[
            pltpu.VMEM((8, 8, LANES), f32),
            pltpu.VMEM((32, 8, LANES), f32),
            pltpu.VMEM((4, 8, LANES), f32),
            pltpu.VMEM((8, 8, LANES), f32),
            pltpu.VMEM((32, 8, LANES), f32),
            pltpu.VMEM((4, 8, 8, LANES), f32),
            pltpu.VMEM((4, 8, LANES), f32),
            pltpu.VMEM((4, 8, 8, LANES), f32),
            pltpu.VMEM((TABLE, 9, 8, LANES), f32),
            pltpu.VMEM((TABLE, 8, 8, LANES), f32),
            pltpu.VMEM((BLOCKS, 9, 16, 8, LANES), f32),
            pltpu.VMEM((BLOCKS, 7, 16, 8, LANES), f32),
            pltpu.VMEM((BLOCKS, BLOCKS, 3, 16, 8, LANES), f32),
            pltpu.VMEM((BLOCKS, 8, LANES), f32),
            pltpu.VMEM((16, 8, LANES), f32),
            pltpu.VMEM(shape, f32),
            pltpu.VMEM((1, LANES), f32),
            pltpu.VMEM((n_slots, 1, LANES), f32),
            dma((4,)), dma((4,)), dma((4,)), dma((4,)), dma((4,)), dma((4,)),
            dma((n_slots,)), dma((n_slots,)),
        ],
        compiler_params=pltpu.CompilerParams(collective_id=0, has_side_effects=True),
        name="sph",
    )(
        positions, velocities, mass.reshape(shape), smoothing.reshape(shape), energy.reshape(shape),
        send_offsets, pair_blocks,
    )
    return dens.reshape(-1), acc, heat.reshape(-1), share.reshape(-1)


def solution(mesh):
    many = P(None, ("slab", "dom"))
    flat = P(("slab", "dom"))
    return jax.shard_map(
        body,
        mesh=mesh,
        in_specs=(many, many, flat, flat, flat, many, many, many),
        out_specs=(flat, many, flat, flat),
        check_vma=False,
    )
```

time: 116 us -> 80.1 us (0.69)
  the two profiles are of different devices: /device:TPU:38 before, /device:TPU:2 now
where the time goes in v2:
time: 80.1 us; the launch traced here: 79.8 us
  Pallas kernels  74.6 us (93%)
  local copies, waits for them, and re-layouts  4.54 us (6%)
    pallas_call x1, Pallas kernels, body(): pl.pallas_call(kernel, out_shape=(jax.ShapeDtypeStruct(shape, f32), jax.S...  74.6 us
    unnamed x13, local copies, waits for them, and re-layouts  4.54 us

profile of v2, /device:TPU:2, one launch (start us, length us, event | category | flops | bytes accessed | tf_op | source)
XLA Modules:
  0.0 79.8 jit_solution(1148885220679309428)
XLA Ops:
  0.6 0.0 copy-start.3
  0.6 0.6 copy-done.3
  1.3 0.7 copy.11.offs
  1.9 74.6 %sph.1 = (f32[8,128]{1,0:T(8,128)}, f32[3,1024]{1,0:T(4,128)}, f32[8,128]{1,0:T(8,128)}, f32[8,128]{1,0:T(8,128)}) custom-call(f32[3,1024]{1,0:T(4,128)} %pos.1, f32[3,1024]{1,0:T(4,128)} %vel.1, f32[8,128]{1,0:T(8,128)} %bitcast.6, f32[8,128]{1,0:T(8,128)} %bitcast.7, f32[8,128]{1,0:T(8,128)} %bitcast.8, s32[4,1]{1,0:T(4,128)} %copy.11.offs, s32[8,8]{1,0:T(8,128)} %pairs.1), custom_call_target="tpu_custom_call" | custom-call | tf_op jit(solution)/shard_map/sph/pallas_call | solution.py:376
  76.6 0.0 copy-start
  76.6 1.3 %copy.16 = f32[1024]{0:T(1024)} copy(f32[1024]{0:T(1024)} %bitcast.11) | data formatting | bytes 8192
  77.9 0.0 copy-done
  77.9 0.0 copy-start.2
  77.9 0.6 copy.17
  78.5 0.1 copy-done.2
  78.6 0.0 copy-start.1
  78.6 0.6 copy.18
  79.2 0.1 copy-done.1
  79.2 0.6 copy.19
Async XLA Ops:
  0.6 0.7 copy-start.3
  76.6 1.3 %copy-start = (f32[3,1024]{1,0:T(4,128)S(1)}, f32[3,1024]{1,0:T(4,128)}, u32[]{:S(2)}) copy-start(f32[3,1024]{1,0:T(4,128)} %get-tuple-element.17) | copy-start | bytes 36868
  77.9 0.7 copy-start.2
  78.6 0.7 copy-start.1
